TPU v7x, 32 devices: a whole 2x2x4 slice. The times are simulated.
32 devices in a mesh: seq: 8 (over z, x), hx: 4 (over y, core).
Axes of the slice: x: 2, y: 2, z: 4, core: 2. Of those that a mesh axis runs over, the one named last changes fastest.
Arguments:
- query: bfloat16 [8192, 8192], P('seq', 'hx'), may hold values from -6 to 6
- key_in: bfloat16 [8192, 8192], P('seq', 'hx'), may hold values from -6 to 6
- value: bfloat16 [8192, 8192], P('seq', 'hx'), may hold values from -6 to 6
- head_gain: float32 [8192], P('hx'), may hold values from 0.1 to 1.9
- out_weight: bfloat16 [8192, 6144], P('hx', 'seq'), may hold values from -0.0625 to 0.0625
- residual: bfloat16 [8192, 6144], P(('seq', 'hx')), may hold values from -6 to 6
Outputs:
- mixed: bfloat16 [8192, 6144], P(('seq', 'hx'))
All inputs are finite; a program needn't handle non-finite values.
Results may differ from a plain program's by a relative error of at most 0.014.
Values may be sent and summed in bfloat16 or wider, within the bound.
A program may use at most 128 MiB of HBM per device.

v0:
```python
import jax
import jax.numpy as jnp
from jax import lax
from jax.sharding import PartitionSpec as P

DH = 128


def entering(x, axis, combine, identity):
    size, position = (lax.axis_size(axis), lax.axis_index(axis))
    everything = lax.all_gather(x.astype(jnp.bfloat16), axis)
    start = jnp.broadcast_to(jnp.asarray(identity, x.dtype), x.shape)

    def turn(k, before):
        reached = k < position
        new = combine(before, everything[k].astype(x.dtype))
        return jnp.where(reached, new, before)

    return lax.fori_loop(0, size, turn, start)


def activate(array):
    return jax.nn.silu(array.astype(jnp.float32)).astype(jnp.bfloat16)


def per_device(query, key_in, value, head_gain, out_weight, residual):
    highest = lax.Precision.HIGHEST
    tokens_here, width = query.shape
    heads = width // DH
    q_act = activate(query).reshape(tokens_here, heads, DH)
    k_act = activate(key_in).reshape(tokens_here, heads, DH)
    v_heads = value.reshape(tokens_here, heads, DH)
    blocks = min(512, tokens_here)
    count = tokens_here // blocks
    rows = jnp.arange(blocks, dtype=jnp.int32)
    lower = rows[:, None] >= rows[None, :]
    running = jnp.zeros((heads, DH, DH), jnp.float32)
    pieces = []
    for index in range(count):
        q_part = q_act[index * blocks : (index + 1) * blocks]
        k_part = k_act[index * blocks : (index + 1) * blocks]
        v_part = v_heads[index * blocks : (index + 1) * blocks]
        scores = jnp.einsum("thd,shd->hts", q_part, k_part, preferred_element_type=jnp.float32)
        scores = jnp.where(lower[None, :, :], scores, jnp.zeros_like(scores))
        inner = jnp.einsum("hts,she->the", scores, v_part.astype(jnp.float32), precision=highest)
        if index > 0:
            inner = inner + jnp.einsum(
                "thd,hde->the", q_part.astype(jnp.float32), running, precision=highest
            )
        pieces.append(inner)
        running = running + jnp.einsum(
            "thd,the->hde", k_part, v_part, preferred_element_type=jnp.float32
        )
    local_part = jnp.concatenate(pieces, axis=0)
    empty = jnp.zeros((heads, DH, DH), jnp.float32)

    def combine(earlier, later):
        return earlier + later

    prefix = entering(running, "seq", combine, empty)
    attended = local_part + jnp.einsum(
        "thd,hde->the", q_act.astype(jnp.float32), prefix, precision=highest
    )
    meansq = jnp.mean(attended * attended, axis=-1, keepdims=True)
    normed = attended * lax.rsqrt(meansq + 1e-06) * head_gain.reshape(heads, DH)
    normed = normed.astype(jnp.bfloat16).reshape(tokens_here, width)
    full_weight = lax.all_gather(out_weight, "seq", axis=1, tiled=True)
    summed = lax.psum_scatter(
        jnp.dot(normed, full_weight, preferred_element_type=jnp.float32).astype(jnp.bfloat16),
        "hx",
        scatter_dimension=0,
        tiled=True,
    ).astype(jnp.float32)
    return (summed + residual.astype(jnp.float32)).astype(jnp.bfloat16)


def solution(mesh):
    return jax.shard_map(
        per_device,
        mesh=mesh,
        in_specs=(
            P("seq", "hx"),
            P("seq", "hx"),
            P("seq", "hx"),
            P("hx"),
            P("hx", "seq"),
            P(("seq", "hx"), None),
        ),
        out_specs=P(("seq", "hx"), None),
        check_vma=False,
    )
```

profile of v0, /device:TPU:0, one launch (start us, length us, event | category | flops | bytes accessed | tf_op | source)
XLA Modules:
  0.0 733.0 jit_solution(13041921529370957699)
XLA Ops:
  6.5 0.0 all-gather.6.cloned.1.call-start
  6.5 6.4 copy.48
  12.9 4.1 fusion.11
  17.0 0.0 copy-start.8
  17.0 2.4 fusion.24
  19.4 1.3 copy-done.8
  20.7 1.8 fusion.23
  22.5 2.5 copy.81
  25.0 2.9 copy.80
  27.9 0.0 copy-start.2
  27.9 0.0 copy-start.3
  27.9 2.4 fusion.27
  30.4 0.0 copy-start.6
  30.4 1.0 copy-done.6
  31.4 0.0 copy-done.2
  31.4 0.0 copy-done.3
  31.4 1.5 fusion.19
  32.9 0.0 all-gather.6.cloned.1.call-update
  32.9 0.0 all-gather.4.cloned.1.call-start
  33.0 0.7 all-gather.4.cloned.1.call-update
  33.7 0.2 reduce-scatter.2.cloned.1.call-start
  33.9 6.4 copy.47
  40.3 0.1 iota_compare_fusion
  40.4 4.1 fusion.7
  44.4 0.0 copy-start
  44.4 0.0 copy-start.4
  44.5 1.6 fusion.22
  46.1 1.2 copy-done
  47.2 0.0 copy-start.5
  47.2 1.3 copy-done.5
  48.6 0.0 copy-done.4
  48.6 2.4 fusion.26
  50.9 11.2 %fusion = f32[16,512,128]{2,1,0:T(8,128)} fusion(bf16[512,16,128]{0,2,1:T(8,128)(2,1)} %bitcast.44, f32[16,512,512]{2,1,0:T(8,128)S(1)} %fusion.26, pred[512,512]{1,0:T(8,128)(4,1)S(1)} %iota_compare_fusion), kind=kOutput, calls=%fused_computation.1 | convolution fusion | flops 6446645248 | bytes 23330816 | tf_op jit(solution)/shard_map/hts,she->the/dot_general | solution.py:45
  62.1 0.0 copy-start.1
  62.1 0.0 copy-start.7
  62.2 7.3 %bitcast_add_fusion = f32[512,16,128]{2,0,1:T(8,128)} fusion(f32[16,512,128]{2,1,0:T(8,128)} %fusion, f32[16,128,128]{2,1,0:T(8,128)} %copy-done.6, bf16[512,16,128]{0,2,1:T(8,128)(2,1)} %bitcast.49), kind=kOutput, calls=%fused_computation.26 | convolution fusion | flops 1611661312 | bytes 11534336 | tf_op jit(solution)/shard_map/thd,hde->the/dot_general | solution.py:47
  69.5 0.0 copy-done.1
  69.5 0.0 copy-done.7
  69.5 2.4 fusion.25
  71.9 10.0 %fusion.16 = f32[512,16,128]{2,0,1:T(8,128)} fusion(bf16[512,16,128]{0,2,1:T(8,128)(2,1)S(1)} %bitcast.41, f32[16,512,512]{2,1,0:T(8,128)S(1)} %fusion.25, pred[512,512]{1,0:T(8,128)(4,1)S(1)} %iota_compare_fusion), kind=kOutput, calls=%fused_computation.27 | convolution fusion | flops 6446645248 | bytes 23330816 | tf_op jit(solution)/shard_map/hts,she->the/dot_general | solution.py:45
  81.8 26.7 %all-gather.6.cloned.1.call-done = bf16[128,128,128]{2,1,0:T(8,128)(2,1)} async-done(((bf16[16,128,128]{2,1,0:T(8,128)(2,1)}), bf16[128,128,128]{2,1,0:T(8,128)(2,1)}) %all-gather.6.cloned.1.call-update) | async-done | bytes 4194320 | tf_op jit(solution)/shard_map/all_gather | solution.py:11
  108.6 13.2 %while.14 = (s32[]{:T(128)}, f32[16,128,128]{2,1,0:T(8,128)S(1)}, s32[]{:T(128)}, bf16[8,16,128,128]{3,2,1,0:T(8,128)(2,1)}, s32[]{:T(128)}, /*index=5*/s32[]{:T(128)}) while((s32[]{:T(128)}, f32[16,128,128]{2,1,0:T(8,128)S(1)}, s32[]{:T(128)}, bf16[8,16,128,128]{3,2,1,0:T(8,128)(2,1)}, s32[]{:T(128)}, /*index=5*/s32[]{:T(128)}) %tuple.45), condition=%wide.region_1.2_spmd.clone, body=%wide.region_0.1_spmd.clone.sunk | while | flops 1048580 | bytes 2621533 | solution.py:19
  108.6 1.6 add_select_fusion.2
  110.2 1.6 add_select_fusion.2
  111.9 1.6 add_select_fusion.2
  113.5 1.6 add_select_fusion.2
  115.1 1.7 add_select_fusion.2
  116.8 1.7 add_select_fusion.2
  118.5 1.6 add_select_fusion.2
  120.2 1.6 add_select_fusion.2
  121.8 0.0 copy-start.10
  121.8 11.0 %multiply_reduce_fusion = (f32[1024,16]{0,1:T(8,128)S(1)}, f32[1024,16,128]{2,0,1:T(8,128)}) fusion(f32[16,128,128]{2,1,0:T(8,128)S(1)} %get-tuple-element.84, bf16[1024,16,128]{0,2,1:T(8,128)(2,1)} %bitcast.39, f32[512,16,128]{2,0,1:T(8,128)} %bitcast_add_fusion, f32[512,16,128]{2,0,1:T(8,128)} %fusion.16), kind=kOutput, calls=%fused_computation.20 | convolution fusion | flops 3229597696 | bytes 22085632 | tf_op jit(solution)/shard_map/thd,hde->the/dot_general | solution.py:61
  132.8 0.0 copy-done.10
  132.8 6.9 multiply_convert_fusion
  139.7 6.4 copy.65
  146.1 442.9 %all-gather.4.cloned.1.call-done = bf16[2048,6144]{1,0:T(8,128)(2,1)} async-done(((bf16[2048,768]{1,0:T(8,128)(2,1)}), bf16[2048,6144]{1,0:T(8,128)(2,1)}) %all-gather.4.cloned.1.call-update) | async-done | bytes 25165840 | tf_op jit(solution)/shard_map/all_gather | solution.py:67
  589.1 32.9 %convolution_convert_fusion = bf16[1024,6144]{1,0:T(8,128)(2,1)} fusion(bf16[1024,2048]{0,1:T(8,128)(2,1)} %bitcast.51, bf16[2048,6144]{1,0:T(8,128)(2,1)} %all-gather.4.cloned.1.call-done), kind=kOutput, calls=%fused_computation.5 | convolution fusion | flops 25776095232 | bytes 41943040 | tf_op jit(solution)/shard_map/dot_general | solution.py:69
  622.0 0.0 copy-start.9
  622.0 0.0 reduce-scatter.2.cloned.1.call-update
  622.0 99.7 %reduce-scatter.2.cloned.1.call-done = bf16[256,6144]{1,0:T(8,128)(2,1)} async-done(((bf16[1024,6144]{1,0:T(8,128)(2,1)}), bf16[256,6144]{1,0:T(8,128)(2,1)}) %reduce-scatter.2.cloned.1.call-update) | async-done | bytes 3145744 | tf_op jit(solution)/shard_map/reduce_scatter | solution.py:68
  721.7 0.0 copy-done.9
  721.7 4.7 add_convert_fusion
  (2 shorter events, 0.0 us)
Async XLA Ops:
  6.5 102.1 %all-gather.6.cloned.1.call-start = ((), (), s32[]{:S(2)}) async-start(), calls=%async_computation.3 | async-start | bytes 4718592 | tf_op jit(solution)/shard_map/all_gather | solution.py:11
  17.0 3.7 copy-start.8
  27.9 3.5 copy-start.2
  27.9 3.5 copy-start.3
  30.4 1.0 copy-start.6
  32.9 556.1 %all-gather.4.cloned.1.call-start = ((), (), s32[]{:S(2)}) async-start(), calls=%async_computation.1 | async-start | bytes 28311552 | tf_op jit(solution)/shard_map/all_gather | solution.py:67
  33.7 688.1 %reduce-scatter.2.cloned.1.call-start = ((), (), s32[]{:S(2)}) async-start(), calls=%async_computation.2 | async-start | bytes 15728640 | tf_op jit(solution)/shard_map/reduce_scatter | solution.py:68
  44.4 2.8 copy-start
  44.4 4.1 copy-start.4
  47.2 1.3 copy-start.5
  62.1 7.4 %copy-start.1 = (bf16[512,2048]{0,1:T(8,128)(2,1)S(1)}, bf16[512,2048]{0,1:T(8,128)(2,1)}, u32[]{:S(2)}) copy-start(bf16[512,2048]{0,1:T(8,128)(2,1)} %get-tuple-element.112) | copy-start | bytes 6291460
  62.1 7.4 %copy-start.7 = (bf16[512,2048]{0,1:T(8,128)(2,1)S(1)}, bf16[512,2048]{0,1:T(8,128)(2,1)}, u32[]{:S(2)}) copy-start(bf16[512,2048]{0,1:T(8,128)(2,1)} %get-tuple-element.108) | copy-start | bytes 6291460
  121.8 11.0 %copy-start.10 = (f32[2048]{0:T(1024)S(1)}, f32[2048]{0:T(1024)}, u32[]{:S(2)}) copy-start(f32[2048]{0:T(1024)} %param.11) | copy-start | bytes 24580
  622.0 99.8 %copy-start.9 = (bf16[256,6144]{1,0:T(8,128)(2,1)S(1)}, bf16[256,6144]{1,0:T(8,128)(2,1)}, u32[]{:S(2)}) copy-start(bf16[256,6144]{1,0:T(8,128)(2,1)} %param.13) | copy-start | bytes 9437188
Sparse Core Ops, SparseCore 0:
  33.0 75.4 all-gather.5
  110.1 478.8 all-gather.3
  622.1 99.5 reduce-scatter.1
where the time goes:
time: 734 us; the launch traced here: 733 us
  waiting for transfers between devices  570 us (78%)
  matrix products  81.1 us (11%)
  local copies, waits for them, and re-layouts  35.2 us (5%)
  other arithmetic  32.9 us (4%)
  between operations  13.3 us (2%)
    all_gather x1, waiting for transfers between devices, per_device(): full_weight = lax.all_gather(out_weight, 'seq', axis=1, tiled=True)  443 us
    reduce_scatter x1, waiting for transfers between devices, per_device(): lax.psum_scatter(jnp.dot(normed, full_weight, preferred_element_type=jnp....  99.7 us
    dot_general x1, matrix products, per_device(): jnp.dot(normed, full_weight, preferred_element_type=jnp.float32)  32.9 us
    all_gather x1, waiting for transfers between devices, entering(): everything = lax.all_gather(x.astype(jnp.bfloat16), axis)  26.7 us
    unnamed x26, local copies, waits for them, and re-layouts  22.9 us
    dot_general x2, matrix products, per_device(): jnp.einsum('hts,she->the', scores, v_part.astype(jnp.float32), precision=...  21.2 us
  transfers between devices with their start and end apart: 3, of which 3 were waited for; matrix products, arithmetic and copies ran while one was open for 11% of the time, Pallas kernels for 0%

commit v1 on v0

--- a/solution.py
+++ b/solution.py
@@ -64,7 +64,26 @@
     meansq = jnp.mean(attended * attended, axis=-1, keepdims=True)
     normed = attended * lax.rsqrt(meansq + 1e-06) * head_gain.reshape(heads, DH)
     normed = normed.astype(jnp.bfloat16).reshape(tokens_here, width)
-    full_weight = lax.all_gather(out_weight, "seq", axis=1, tiled=True)
+    size_2, place, extent = (lax.axis_size("seq"), lax.axis_index("seq"), out_weight.shape[1])
+    right = [(i, (i + 1) % size_2) for i in range(size_2)]
+    downward = [(i, (i - 1) % size_2) for i in range(size_2)]
+    whole = jnp.zeros(
+        (*out_weight.shape[:1], size_2 * extent, *out_weight.shape[1 + 1 :]), out_weight.dtype
+    )
+    whole = lax.dynamic_update_slice_in_dim(whole, out_weight, place * extent, axis=1)
+    from_left = from_right = out_weight
+    half = size_2 // 2
+    for step in range(1, half + 1):
+        from_left = lax.ppermute(from_left, "seq", right)
+        whole = lax.dynamic_update_slice_in_dim(
+            whole, from_left, (place - step) % size_2 * extent, axis=1
+        )
+        if step < size_2 - half:
+            from_right = lax.ppermute(from_right, "seq", downward)
+            whole = lax.dynamic_update_slice_in_dim(
+                whole, from_right, (place + step) % size_2 * extent, axis=1
+            )
+    full_weight = whole
     summed = lax.psum_scatter(
         jnp.dot(normed, full_weight, preferred_element_type=jnp.float32).astype(jnp.bfloat16),
         "hx",

time: 734 us -> 670 us (0.913)
  waiting for transfers between devices: 570 us -> 440 us
  local copies, waits for them, and re-layouts: 35.2 us -> 76.4 us
  starting transfers between devices: 0.26 us -> 20.3 us
    all_gather x1 -> x0, waiting for transfers between devices: 443 us -> none  [per_device(): full_weight = lax.all_gather(out_weight, 'seq', axis=1, tiled=True)]
    ppermute x0 -> x7, waiting for transfers between devices: none -> 342 us  [the longest x4 342 us: per_device(): from_left = lax.ppermute(from_left, 'seq', right)]
    dynamic_update_slice x0 -> x8, local copies, waits for them, and re-layouts: none -> 27.3 us  [the longest x4 15.4 us: per_device(): lax.dynamic_update_slice_in_dim(whole, from_left, (place - step) % size_2...]
    all_gather x1, waiting for transfers between devices: 26.7 us -> 0.01 us  [entering(): everything = lax.all_gather(x.astype(jnp.bfloat16), axis)]
    ppermute x0 -> x7, starting transfers between devices: none -> 20.3 us  [the longest x4 11.2 us: per_device(): from_left = lax.ppermute(from_left, 'seq', right)]
    unnamed x26 -> x22, local copies, waits for them, and re-layouts: 22.9 us -> 29.4 us
  transfers between devices with their start and end apart: 3 -> 9, of which waited for: 3 -> 5; matrix products, arithmetic and copies ran while one was open for 11% -> 21% of each run, Pallas kernels for 0% -> 0%
where the time goes in v1:
time: 670 us; the launch traced here: 665 us
  waiting for transfers between devices  440 us (66%)
  matrix products  81.8 us (12%)
  local copies, waits for them, and re-layouts  76.4 us (11%)
  other arithmetic  32.1 us (5%)
  starting transfers between devices  20.3 us (3%)
  between operations  13.8 us (2%)
    ppermute x4, waiting for transfers between devices, per_device(): from_left = lax.ppermute(from_left, 'seq', right)  342 us
    reduce_scatter x1, waiting for transfers between devices, per_device(): lax.psum_scatter(jnp.dot(normed, full_weight, preferred_element_type=jnp....  98.1 us
    dot_general x1, matrix products, per_device(): jnp.dot(normed, full_weight, preferred_element_type=jnp.float32)  32.4 us
    unnamed x22, local copies, waits for them, and re-layouts  29.4 us
    dot_general x2, matrix products, per_device(): jnp.einsum('hts,she->the', scores, v_part.astype(jnp.float32), precision=...  21.2 us
    dynamic_update_slice x4, local copies, waits for them, and re-layouts, per_device(): lax.dynamic_update_slice_in_dim(whole, from_left, (place - step) % size_2...  15.4 us
  transfers between devices with their start and end apart: 9, of which 5 were waited for; matrix products, arithmetic and copies ran while one was open for 21% of the time, Pallas kernels for 0%

profile of v1, /device:TPU:0, one launch (start us, length us, event | category | flops | bytes accessed | tf_op | source)
XLA Modules:
  0.0 664.6 jit_solution(3450283047148660956)
XLA Ops:
  6.5 3.0 collective-permute-start
  9.5 3.0 collective-permute-start.1
  12.5 6.4 copy.48
  18.9 4.8 fusion.23
  23.7 2.9 copy.80
  26.6 3.9 copy.81
  30.5 4.1 fusion.11
  34.6 1.6 fusion.24
  36.2 3.1 fusion.27
  39.3 1.5 fusion.19
  40.9 0.0 all-gather.3.cloned.1.call-update
  40.9 0.0 reduce-scatter.2.cloned.1.call-start
  41.0 6.5 copy.47
  47.4 0.0 copy-done.5
  47.4 125.3 %collective-permute-done = bf16[2048,768]{1,0:T(8,128)(2,1)} collective-permute-done((bf16[2048,768]{1,0:T(8,128)(2,1)}, bf16[2048,768]{1,0:T(8,128)(2,1)}, u32[]{:S(2)}, u32[]{:S(2)}) %collective-permute-start) | collective-permute-done | bytes 3145760 | tf_op jit(solution)/shard_map/ppermute | solution.py:77
  172.7 2.9 collective-permute-start.2
  175.6 5.4 fusion.7
  181.0 0.1 iota_compare_fusion
  181.1 0.0 copy-start.3
  181.1 3.9 fusion.22
  185.1 1.4 copy-done.4
  186.4 0.0 copy-done.3
  186.4 2.4 fusion.26
  188.8 11.3 %fusion = f32[16,512,128]{2,1,0:T(8,128)} fusion(bf16[512,16,128]{0,2,1:T(8,128)(2,1)} %bitcast.42, f32[16,512,512]{2,1,0:T(8,128)S(1)} %fusion.26, pred[512,512]{1,0:T(8,128)(4,1)S(1)} %iota_compare_fusion), kind=kOutput, calls=%fused_computation.1 | convolution fusion | flops 6446645248 | bytes 23330816 | tf_op jit(solution)/shard_map/hts,she->the/dot_general | solution.py:45
  200.1 0.0 collective-permute-done.1
  200.1 3.1 collective-permute-start.3
  203.2 7.3 %bitcast_add_fusion = f32[512,16,128]{2,0,1:T(8,128)} fusion(f32[16,512,128]{2,1,0:T(8,128)} %fusion, f32[16,128,128]{2,1,0:T(8,128)} %copy-done.5, bf16[512,16,128]{0,2,1:T(8,128)(2,1)} %bitcast.47), kind=kOutput, calls=%fused_computation.26 | convolution fusion | flops 1611661312 | bytes 11534336 | tf_op jit(solution)/shard_map/thd,hde->the/dot_general | solution.py:47
  210.5 99.3 %collective-permute-done.2 = bf16[2048,768]{1,0:T(8,128)(2,1)} collective-permute-done((bf16[2048,768]{1,0:T(8,128)(2,1)}, bf16[2048,768]{1,0:T(8,128)(2,1)}, u32[]{:S(2)}, u32[]{:S(2)}) %collective-permute-start.2) | collective-permute-done | bytes 3145760 | tf_op jit(solution)/shard_map/ppermute | solution.py:77
  309.8 2.6 collective-permute-start.4
  312.5 3.1 broadcast_in_dim.26
  315.5 0.4 constant_dynamic-update-slice_fusion.7
  316.0 8.3 %copy-done = bf16[2048,6144]{1,0:T(8,128)(2,1)} copy-done((bf16[2048,6144]{1,0:T(8,128)(2,1)}, bf16[2048,6144]{1,0:T(8,128)(2,1)S(1)}, u32[]{:S(2)}) %copy-start) | copy-done | bytes 25165848
  324.3 4.6 fusion.25
  328.9 9.9 %fusion.16 = f32[512,16,128]{2,0,1:T(8,128)} fusion(bf16[512,16,128]{0,2,1:T(8,128)(2,1)S(1)} %bitcast.41, f32[16,512,512]{2,1,0:T(8,128)S(1)} %fusion.25, pred[512,512]{1,0:T(8,128)(4,1)S(1)} %iota_compare_fusion), kind=kOutput, calls=%fused_computation.27 | convolution fusion | flops 6446645248 | bytes 23330816 | tf_op jit(solution)/shard_map/hts,she->the/dot_general | solution.py:45
  338.8 3.9 constant_dynamic-update-slice_fusion.6
  342.7 3.8 constant_dynamic-update-slice_fusion.5
  346.5 0.0 collective-permute-done.3
  346.5 3.0 collective-permute-start.5
  349.4 3.8 constant_dynamic-update-slice_fusion.4
  353.2 3.9 constant_dynamic-update-slice_fusion.3
  357.1 88.8 %collective-permute-done.4 = bf16[2048,768]{1,0:T(8,128)(2,1)} collective-permute-done((bf16[2048,768]{1,0:T(8,128)(2,1)}, bf16[2048,768]{1,0:T(8,128)(2,1)}, u32[]{:S(2)}, u32[]{:S(2)}) %collective-permute-start.4) | collective-permute-done | bytes 3145760 | tf_op jit(solution)/shard_map/ppermute | solution.py:77
  445.8 2.7 collective-permute-start.6
  448.5 13.1 %while.14 = (s32[]{:T(128)}, f32[16,128,128]{2,1,0:T(8,128)S(1)}, s32[]{:T(128)}, bf16[8,16,128,128]{3,2,1,0:T(8,128)(2,1)}, s32[]{:T(128)}, /*index=5*/s32[]{:T(128)}) while((s32[]{:T(128)}, f32[16,128,128]{2,1,0:T(8,128)S(1)}, s32[]{:T(128)}, bf16[8,16,128,128]{3,2,1,0:T(8,128)(2,1)}, s32[]{:T(128)}, /*index=5*/s32[]{:T(128)}) %tuple.43), condition=%wide.region_1.2_spmd.clone, body=%wide.region_0.1_spmd.clone.sunk | while | flops 1048580 | bytes 2621541 | solution.py:19
  448.5 1.6 add_select_fusion.2
  450.2 1.6 add_select_fusion.2
  451.8 1.6 add_select_fusion.2
  453.4 1.6 add_select_fusion.2
  455.1 1.6 add_select_fusion.2
  456.7 1.6 add_select_fusion.2
  458.4 1.6 add_select_fusion.2
  460.0 1.6 add_select_fusion.2
  461.6 0.0 copy-start.8
  461.6 9.3 %multiply_reduce_fusion = (f32[1024,16]{0,1:T(8,128)S(1)}, f32[1024,16,128]{2,0,1:T(8,128)S(1)}) fusion(f32[16,128,128]{2,1,0:T(8,128)S(1)} %get-tuple-element.84, bf16[1024,16,128]{0,2,1:T(8,128)(2,1)} %bitcast.39, f32[512,16,128]{2,0,1:T(8,128)} %bitcast_add_fusion, f32[512,16,128]{2,0,1:T(8,128)} %fusion.16), kind=kOutput, calls=%fused_computation.20 | convolution fusion | flops 3229597696 | bytes 22085632 | tf_op jit(solution)/shard_map/thd,hde->the/dot_general | solution.py:61
  470.9 3.9 multiply_convert_fusion
  474.8 6.3 copy.65
  481.2 3.9 constant_dynamic-update-slice_fusion.2
  485.1 0.0 collective-permute-done.5
  485.1 3.8 constant_dynamic-update-slice_fusion.1
  488.9 28.5 %collective-permute-done.6 = bf16[2048,768]{1,0:T(8,128)(2,1)} collective-permute-done((bf16[2048,768]{1,0:T(8,128)(2,1)}, bf16[2048,768]{1,0:T(8,128)(2,1)}, u32[]{:S(2)}, u32[]{:S(2)}) %collective-permute-start.6) | collective-permute-done | bytes 3145760 | tf_op jit(solution)/shard_map/ppermute | solution.py:77
  517.4 3.9 constant_dynamic-update-slice_fusion
  521.3 32.4 %convolution_convert_fusion = bf16[1024,6144]{1,0:T(8,128)(2,1)} fusion(bf16[1024,2048]{0,1:T(8,128)(2,1)S(1)} %bitcast.49, bf16[2048,6144]{1,0:T(8,128)(2,1)} %constant_dynamic-update-slice_fusion), kind=kOutput, calls=%fused_computation.5 | convolution fusion | flops 25776095232 | bytes 41943040 | tf_op jit(solution)/shard_map/dot_general | solution.py:88
  553.7 0.0 reduce-scatter.2.cloned.1.call-update
  553.7 98.1 %reduce-scatter.2.cloned.1.call-done = bf16[256,6144]{1,0:T(8,128)(2,1)} async-done(((bf16[1024,6144]{1,0:T(8,128)(2,1)}), bf16[256,6144]{1,0:T(8,128)(2,1)}) %reduce-scatter.2.cloned.1.call-update) | async-done | bytes 3145744 | tf_op jit(solution)/shard_map/reduce_scatter | solution.py:87
  651.9 5.7 add_convert_fusion
  (16 shorter events, 0.0 us)
Async XLA Ops:
  6.5 442.0 %all-gather.3.cloned.1.call-start = ((), (), s32[]{:S(2)}) async-start(), calls=%async_computation.2 | async-start | bytes 4718592 | tf_op jit(solution)/shard_map/all_gather | solution.py:11
  6.5 166.1 %collective-permute-start = (bf16[2048,768]{1,0:T(8,128)(2,1)}, bf16[2048,768]{1,0:T(8,128)(2,1)}, u32[]{:S(2)}, u32[]{:S(2)}) collective-permute-start(bf16[2048,768]{1,0:T(8,128)(2,1)} %param.12), channel_id=1, source_target_pairs={{0,4},{4,8},{8,12},{12,16},{16,20},{20,24},{24,28},{28,0},{1,5},{5... | collective-permute-start | bytes 9437192 | tf_op jit(solution)/shard_map/ppermute | solution.py:77
  9.5 190.6 %collective-permute-start.1 = (bf16[2048,768]{1,0:T(8,128)(2,1)}, bf16[2048,768]{1,0:T(8,128)(2,1)}, u32[]{:S(2)}, u32[]{:S(2)}) collective-permute-start(bf16[2048,768]{1,0:T(8,128)(2,1)} %param.12), channel_id=1, source_target_pairs={{0,28},{4,0},{8,4},{12,8},{16,12},{20,16},{24,20},{28,24},{1,29},{... | collective-permute-start | bytes 9437192 | tf_op jit(solution)/shard_map/ppermute | solution.py:82
  36.2 3.1 copy-start.2
  36.2 3.1 copy-start.1
  39.3 8.1 %copy-start.5 = (f32[16,128,128]{2,1,0:T(8,128)}, f32[16,128,128]{2,1,0:T(8,128)S(1)}, u32[]{:S(2)}) copy-start(f32[16,128,128]{2,1,0:T(8,128)S(1)} %fusion.27) | copy-start | bytes 3145732
  40.9 611.0 %reduce-scatter.2.cloned.1.call-start = ((), (), s32[]{:S(2)}) async-start(), calls=%async_computation.1 | async-start | bytes 15728640 | tf_op jit(solution)/shard_map/reduce_scatter | solution.py:87
  172.7 137.2 %collective-permute-start.2 = (bf16[2048,768]{1,0:T(8,128)(2,1)}, bf16[2048,768]{1,0:T(8,128)(2,1)}, u32[]{:S(2)}, u32[]{:S(2)}) collective-permute-start(bf16[2048,768]{1,0:T(8,128)(2,1)} %collective-permute-done), channel_id=1, source_target_pairs={{0,4},{4,8},{8,12},{12,16},{16,20},{20,24},{24,28},{28,0},{1,5},{5... | collective-permute-start | bytes 9437192 | tf_op jit(solution)/shard_map/ppermute | solution.py:77
  181.1 5.3 copy-start.3
  185.1 1.4 copy-start.4
  200.1 146.4 %collective-permute-start.3 = (bf16[2048,768]{1,0:T(8,128)(2,1)}, bf16[2048,768]{1,0:T(8,128)(2,1)}, u32[]{:S(2)}, u32[]{:S(2)}) collective-permute-start(bf16[2048,768]{1,0:T(8,128)(2,1)} %collective-permute-done.1), channel_id=1, source_target_pairs={{0,28},{4,0},{8,4},{12,8},{16,12},{20,16},{24,20},{28,24},{1,29},{... | collective-permute-start | bytes 9437192 | tf_op jit(solution)/shard_map/ppermute | solution.py:82
  210.5 105.0 %copy-start.7 = (bf16[2048,768]{1,0:T(8,128)(2,1)S(1)}, bf16[2048,768]{1,0:T(8,128)(2,1)}, u32[]{:S(2)}) copy-start(bf16[2048,768]{1,0:T(8,128)(2,1)} %param.12) | copy-start | bytes 9437188
  309.8 136.0 %collective-permute-start.4 = (bf16[2048,768]{1,0:T(8,128)(2,1)}, bf16[2048,768]{1,0:T(8,128)(2,1)}, u32[]{:S(2)}, u32[]{:S(2)}) collective-permute-start(bf16[2048,768]{1,0:T(8,128)(2,1)} %collective-permute-done.2), channel_id=1, source_target_pairs={{0,4},{4,8},{8,12},{12,16},{16,20},{20,24},{24,28},{28,0},{1,5},{5... | collective-permute-start | bytes 9437192 | tf_op jit(solution)/shard_map/ppermute | solution.py:77
  316.0 8.3 %copy-start = (bf16[2048,6144]{1,0:T(8,128)(2,1)}, bf16[2048,6144]{1,0:T(8,128)(2,1)S(1)}, u32[]{:S(2)}) copy-start(bf16[2048,6144]{1,0:T(8,128)(2,1)S(1)} %constant_dynamic-update-slice_fusion.7) | copy-start | bytes 75497472
  346.5 138.6 %collective-permute-start.5 = (bf16[2048,768]{1,0:T(8,128)(2,1)}, bf16[2048,768]{1,0:T(8,128)(2,1)}, u32[]{:S(2)}, u32[]{:S(2)}) collective-permute-start(bf16[2048,768]{1,0:T(8,128)(2,1)} %collective-permute-done.3), channel_id=1, source_target_pairs={{0,28},{4,0},{8,4},{12,8},{16,12},{20,16},{24,20},{28,24},{1,29},{... | collective-permute-start | bytes 9437192 | tf_op jit(solution)/shard_map/ppermute | solution.py:82
  445.8 71.6 %collective-permute-start.6 = (bf16[2048,768]{1,0:T(8,128)(2,1)}, bf16[2048,768]{1,0:T(8,128)(2,1)}, u32[]{:S(2)}, u32[]{:S(2)}) collective-permute-start(bf16[2048,768]{1,0:T(8,128)(2,1)} %collective-permute-done.4), channel_id=1, source_target_pairs={{0,4},{4,8},{8,12},{12,16},{16,20},{20,24},{24,28},{28,0},{1,5},{5... | collective-permute-start | bytes 9437192 | tf_op jit(solution)/shard_map/ppermute | solution.py:77
  461.6 9.3 %copy-start.8 = (f32[2048]{0:T(1024)S(1)}, f32[2048]{0:T(1024)}, u32[]{:S(2)}) copy-start(f32[2048]{0:T(1024)} %param.11) | copy-start | bytes 24580
  488.9 32.4 %copy-start.6 = (bf16[1024,16,128]{0,2,1:T(8,128)(2,1)S(1)}, bf16[1024,16,128]{0,2,1:T(8,128)(2,1)}, u32[]{:S(2)}) copy-start(bf16[1024,16,128]{0,2,1:T(8,128)(2,1)} %copy.65) | copy-start | bytes 12582916
Sparse Core Ops, SparseCore 0:
  41.0 128.9 all-gather.2
  553.8 97.9 reduce-scatter.1
